TPU v7x, 128 devices: a whole 4x4x4 slice. The times are simulated.
128 devices in a mesh: gy: 32 (over z, y, core), var: 4 (over x).
Axes of the slice: x: 4, y: 4, z: 4, core: 2. Of those that a mesh axis runs over, the one named last changes fastest.
Arguments:
- field: float32 [32, 32, 1024, 128], P('var', None, 'gy')
- factor_x: float32 [32, 16], replicated, may hold values from -1 to 1
- factor_y: float32 [1024, 64], P('gy'), may hold values from -0.1875 to 0.1875
- factor_z: float32 [128, 64], replicated, may hold values from -0.5 to 0.5
- factor_v: float32 [32, 16], replicated, may hold values from -1 to 1
Outputs:
- proj_z: float32 [128, 128], replicated
- proj_v: float32 [32, 32], replicated
- core_rms: float32 [], replicated
All inputs are finite; a program needn't handle non-finite values.
Results may differ from a plain program's by a relative error of at most 0.0003.
Values sent between devices are 32-bit elements; how exact they have to be, the bound alone decides.
No kernel may reach another device: no remote copies, remote signals or barrier semaphores. Data moves between devices by JAX's collectives and lax.ppermute only.
A program may use at most 192 MiB of HBM per device.

v0:
```python
import jax
import jax.numpy as jnp
from jax import lax
from jax.sharding import PartitionSpec as P

precise = lax.Precision.HIGHEST


def orth(mat):
    gram = jnp.dot(mat.T, mat, precision=precise)
    lower = jnp.linalg.cholesky(gram)
    return jax.scipy.linalg.solve_triangular(lower, mat.T, lower=True).T


def total_core(local_part):
    return lax.psum(local_part, ("gy", "var"))


def per_device(field, factor_x, factor_y, factor_z, factor_v):
    var_rows = field.shape[0]
    var_start = lax.axis_index("var") * var_rows
    local_v = lax.dynamic_slice_in_dim(factor_v, var_start, var_rows, 0)
    along_x = jnp.einsum("vxyz,xa->vayz", field, factor_x, precision=precise)
    partial_value = jnp.einsum("vayz,yb->vabz", along_x, factor_y, precision=precise)
    wide_z = jnp.einsum("vabz,vc->cabz", partial_value, local_v, precision=precise)
    fibres = lax.psum_scatter(wide_z, ("gy", "var"), scatter_dimension=3, tiled=True)
    z_count = fibres.shape[3]
    z_start = lax.axis_index(("gy", "var")) * z_count
    local_z = lax.dynamic_slice_in_dim(factor_z, z_start, z_count, 0)
    small_core = total_core(jnp.einsum("cabz,zr->cabr", fibres, local_z, precision=precise))
    rows_z = jnp.einsum("cabz,cabr->zr", fibres, small_core, precision=precise)
    raw_z = lax.all_gather(rows_z, ("gy", "var"), axis=0, tiled=True)
    new_z = orth(raw_z)
    proj_z = jnp.dot(new_z, new_z.T, precision=precise)
    wide_v = jnp.einsum("vabz,zr->vabr", partial_value, new_z, precision=precise)
    flat_v = wide_v.reshape(var_rows, -1)
    summed_v = lax.psum(flat_v, "gy")
    every_v = lax.all_gather(summed_v, "var", axis=0, tiled=True)
    gram_v = jnp.dot(every_v, every_v.T, precision=precise)
    new_v = orth(jnp.dot(gram_v, factor_v, precision=precise))
    proj_v = jnp.dot(new_v, new_v.T, precision=precise)
    core = jnp.dot(new_v.T, every_v, precision=precise)
    core_rms = jnp.sqrt(jnp.mean(core * core))
    return (proj_z, proj_v, core_rms)


def solution(mesh):
    in_specs = (P("var", None, "gy", None), P(), P("gy", None), P(), P())
    out_specs = (P(), P(), P())
    return jax.shard_map(
        per_device, mesh=mesh, in_specs=in_specs, out_specs=out_specs, check_vma=False
    )
```

profile of v0, /device:TPU:1, one launch (start us, length us, event | category | flops | bytes accessed | tf_op | source)
XLA Modules:
  0.0 1346.6 jit_solution(12369558590492828368)
XLA Ops:
  7.2 6.9 fusion.5
  14.1 4.1 convolution_bitcast_fusion
  18.2 2.0 copy-done.1
  20.2 5.2 copy.21
  25.4 122.6 %fusion.25 = f32[16,131072]{0,1} fusion(f32[8,131072]{1,0:T(8,128)} %bitcast.65, f32[32,16]{0,1:T(8,128)S(1)} %copy-done.3, s32[]{:T(128)S(6)} %select_n.14), kind=kOutput, calls=%fused_computation.35 | convolution fusion | flops 201326592 | bytes 71305216
  148.0 42.6 %copy.22 = f32[16,16,64,128]{2,1,0,3:T(8,128)} copy(f32[16,16,64,128]{0,3,2,1:T(8,128)} %bitcast.7) | data formatting | bytes 16777216 | tf_op jit(solution)/shard_map/vabz,vc->cabz/dot_general | solution.py:25
  190.8 0.2 dynamic-slice_reduce_fusion
  190.9 668.2 %reduce-scatter.2.cloned.1.call-done = f32[16,16,64,1]{2,1,0,3:T(8,128)} async-done(((f32[16,16,64,128]{2,1,0,3:T(8,128)}), f32[16,16,64,1]{2,1,0,3:T(8,128)}) %reduce-scatter.2.cloned.1.call-update) | async-done | bytes 65552 | tf_op jit(solution)/shard_map/reduce_scatter | solution.py:26
  859.1 5.5 broadcast_multiply_fusion
  864.7 165.4 %all-reduce.4.cloned.1.call-done = f32[16,16,64,64]{3,2,1,0:T(8,128)} async-done(((f32[16,16,64,64]{3,2,1,0:T(8,128)}), f32[16,16,64,64]{3,2,1,0:T(8,128)}) %all-reduce.4.cloned.1.call-update) | async-done | bytes 4194320 | tf_op jit(solution)/shard_map/psum | solution.py:16
  1030.1 6.6 fusion.9
  1036.8 0.3 dynamic-update-slice.6
  1037.0 64.0 %all-reduce = f32[8192]{0:T(1024)S(1)} all-reduce(f32[8192]{0:T(1024)S(1)} %dynamic-update-slice.6), channel_id=2, replica_groups=mesh['gy'=32,'var'=4] {'gy','var'}, use_global_device_ids=true, to_apply=%add | all-reduce | flops 8192 | bytes 65536
  1101.2 0.3 fusion.28
  1101.5 5.8 cholesky.29
  1107.4 0.6 compare_reduce_fusion.1
  1108.0 0.7 fusion.13
  1108.7 4.9 custom-call.14
  1113.6 0.3 fusion.16
  1113.9 6.6 fusion.14
  1120.5 4.7 reshape.38
  1125.3 104.6 %all-reduce.6.cloned.1.call-done = f32[8,65536]{1,0:T(8,128)} async-done(((f32[8,65536]{1,0:T(8,128)}), f32[8,65536]{1,0:T(8,128)}) %all-reduce.6.cloned.1.call-update) | async-done | bytes 2097168 | tf_op jit(solution)/shard_map/psum | solution.py:37
  1229.9 0.9 fusion.29
  1230.8 83.4 %all-gather.3.cloned.1.call-done = f32[32,65536]{1,0:T(8,128)} async-done(((f32[8,65536]{1,0:T(8,128)}), f32[32,65536]{1,0:T(8,128)}) %all-gather.3.cloned.1.call-update) | async-done | bytes 8388624 | tf_op jit(solution)/shard_map/all_gather | solution.py:38
  1314.2 10.7 fusion.30
  1325.2 1.5 cholesky.61
  1326.7 0.6 compare_reduce_fusion
  1327.4 0.6 fusion.20
  1328.0 1.2 custom-call.15
  1329.3 0.2 fusion.22
  1329.5 0.8 fusion.33
  1330.3 7.5 fusion.8
  (27 shorter events, 0.8 us)
Async XLA Ops:
  7.2 183.6 %copy-start = (f32[128,64]{0,1:T(8,128)S(1)}, f32[128,64]{0,1:T(8,128)}, u32[]{:S(2)}) copy-start(f32[128,64]{0,1:T(8,128)} %param.8) | copy-start | bytes 98308
  7.2 6.9 copy-start.4
  7.2 851.9 %reduce-scatter.2.cloned.1.call-start = ((), (), s32[]{:S(2)}) async-start(), calls=%async_computation.1 | async-start | bytes 16908288 | tf_op jit(solution)/shard_map/reduce_scatter | solution.py:26
  18.2 2.0 copy-start.1
  20.2 5.3 copy-start.3
  190.7 839.4 %all-reduce.4.cloned.1.call-start = ((), (), s32[]{:S(2)}) async-start(), calls=%async_computation.2 | async-start | bytes 16777216 | tf_op jit(solution)/shard_map/psum | solution.py:16
  864.6 165.5 %copy-start.2 = (f32[16,16,64,1]{2,1,0,3:T(8,128)S(1)}, f32[16,16,64,1]{2,1,0,3:T(8,128)}, u32[]{:S(2)}) copy-start(f32[16,16,64,1]{2,1,0,3:T(8,128)} %reduce-scatter.2.cloned.1.call-done) | copy-start | bytes 196612
  864.6 365.3 %all-reduce.6.cloned.1.call-start = ((), (), s32[]{:S(2)}) async-start(), calls=%async_computation.3 | async-start | bytes 4194304 | tf_op jit(solution)/shard_map/psum | solution.py:37
  1125.2 189.0 %all-gather.3.cloned.1.call-start = ((), (), s32[]{:S(2)}) async-start(), calls=%async_computation.4 | async-start | bytes 10485760 | tf_op jit(solution)/shard_map/all_gather | solution.py:38
Sparse Core Ops, SparseCore 0:
  190.8 668.2 reduce-scatter.1
  864.7 165.3 all-reduce.3
  1125.3 104.5 all-reduce.5
  1231.5 82.6 all-gather.2
where the time goes:
time: 1350 us
  waiting for transfers between devices  1020 us (76%)
  matrix products  168 us (12%)
  blocking collectives  64 us (5%)
  local copies, waits for them, and re-layouts  55.3 us (4%)
  other arithmetic  21.6 us (2%)
  between operations  16.2 us (1%)
    reduce_scatter x1, waiting for transfers between devices, per_device(): lax.psum_scatter(wide_z, ('gy', 'var'), scatter_dimension=3, tiled=True)  668 us
    psum x1, waiting for transfers between devices, total_core(): return lax.psum(local_part, ('gy', 'var'))  165 us
    unnamed x1, matrix products  123 us
    psum x1, waiting for transfers between devices, per_device(): summed_v = lax.psum(flat_v, 'gy')  105 us
    all_gather x1, waiting for transfers between devices, per_device(): every_v = lax.all_gather(summed_v, 'var', axis=0, tiled=True)  83.4 us
    unnamed x1, blocking collectives  64 us
    dot_general x1, local copies, waits for them, and re-layouts, per_device(): jnp.einsum('vabz,vc->cabz', partial_value, local_v, precision=precise)  42.6 us
  transfers between devices with their start and end apart: 4, of which 4 were waited for; matrix products, arithmetic and copies ran while one was open for 0% of the time, Pallas kernels for 0%

commit v1 on v0

--- a/solution.py
+++ b/solution.py
@@ -4,6 +4,22 @@
 from jax.sharding import PartitionSpec as P
 
 precise = lax.Precision.HIGHEST
+
+
+def ring_gather(x, axis, dim):
+    ways, here, hop = (lax.axis_size(axis), lax.axis_index(axis), x.shape[dim])
+    dims = [n * ways if d == dim else n for d, n in enumerate(x.shape)]
+    full = lax.dynamic_update_slice_in_dim(jnp.zeros(dims, x.dtype), x, here * hop, axis=dim)
+    going_up = going_down = x
+    for far in range(1, ways // 2 + 1):
+        going_up = lax.ppermute(going_up, axis, [(d, (d + 1) % ways) for d in range(ways)])
+        full = lax.dynamic_update_slice_in_dim(full, going_up, (here - far) % ways * hop, axis=dim)
+        if 2 * far < ways:
+            going_down = lax.ppermute(going_down, axis, [(d, (d - 1) % ways) for d in range(ways)])
+            full = lax.dynamic_update_slice_in_dim(
+                full, going_down, (here + far) % ways * hop, axis=dim
+            )
+    return full
 
 
 def orth(mat):
@@ -35,7 +51,7 @@
     wide_v = jnp.einsum("vabz,zr->vabr", partial_value, new_z, precision=precise)
     flat_v = wide_v.reshape(var_rows, -1)
     summed_v = lax.psum(flat_v, "gy")
-    every_v = lax.all_gather(summed_v, "var", axis=0, tiled=True)
+    every_v = ring_gather(summed_v, "var", 0)
     gram_v = jnp.dot(every_v, every_v.T, precision=precise)
     new_v = orth(jnp.dot(gram_v, factor_v, precision=precise))
     proj_v = jnp.dot(new_v, new_v.T, precision=precise)

time: 1350 us -> 1350 us (level)
  matrix products: 168 us -> 153 us
    ppermute x0 -> x3, waiting for transfers between devices: none -> 90.8 us  [the longest x2 90.8 us: ring_gather(): lax.ppermute(going_up, axis, [(d, (d + 1) % ways) for d in range(ways)])]
    all_gather x1 -> x0, waiting for transfers between devices: 83.4 us -> none  [per_device(): every_v = lax.all_gather(summed_v, 'var', axis=0, tiled=True)]
  transfers between devices with their start and end apart: 4 -> 6, of which waited for: 4 -> 5; matrix products, arithmetic and copies ran while one was open for 0% -> 0% of each run, Pallas kernels for 0% -> 0%
where the time goes in v1:
time: 1350 us; the launch traced here: 1340 us
  waiting for transfers between devices  1030 us (76%)
  matrix products  153 us (11%)
  blocking collectives  64.1 us (5%)
  local copies, waits for them, and re-layouts  56.6 us (4%)
  other arithmetic  21.7 us (2%)
  between operations  16 us (1%)
    reduce_scatter x1, waiting for transfers between devices, per_device(): lax.psum_scatter(wide_z, ('gy', 'var'), scatter_dimension=3, tiled=True)  667 us
    psum x1, waiting for transfers between devices, total_core(): return lax.psum(local_part, ('gy', 'var'))  166 us
    unnamed x1, matrix products  111 us
    psum x1, waiting for transfers between devices, per_device(): summed_v = lax.psum(flat_v, 'gy')  104 us
    ppermute x2, waiting for transfers between devices, ring_gather(): lax.ppermute(going_up, axis, [(d, (d + 1) % ways) for d in range(ways)])  90.8 us
    unnamed x1, blocking collectives  64.1 us
    dot_general x1, local copies, waits for them, and re-layouts, per_device(): jnp.einsum('vabz,vc->cabz', partial_value, local_v, precision=precise)  42.7 us
  transfers between devices with their start and end apart: 6, of which 5 were waited for; matrix products, arithmetic and copies ran while one was open for 0% of the time, Pallas kernels for 0%

profile of v1, /device:TPU:1, one launch (start us, length us, event | category | flops | bytes accessed | tf_op | source)
XLA Modules:
  0.0 1342.2 jit_solution(9474778738446365874)
XLA Ops:
  7.2 6.9 fusion.5
  14.1 4.8 convolution_bitcast_fusion
  18.9 2.0 copy-done.2
  20.9 5.2 copy.21
  26.2 111.2 %fusion.25 = f32[16,131072]{0,1} fusion(f32[8,131072]{1,0:T(8,128)} %bitcast.65, f32[32,16]{0,1:T(8,128)S(1)} %copy-done.5, s32[]{:T(128)S(6)} %select_n.39), kind=kOutput, calls=%fused_computation.35 | convolution fusion | flops 201326592 | bytes 71305216
  137.3 42.7 %copy.22 = f32[16,16,64,128]{2,1,0,3:T(8,128)} copy(f32[16,16,64,128]{0,3,2,1:T(8,128)} %bitcast.7) | data formatting | bytes 16777216 | tf_op jit(solution)/shard_map/vabz,vc->cabz/dot_general | solution.py:41
  180.3 667.3 %reduce-scatter.2.cloned.1.call-done = f32[16,16,64,1]{2,1,0,3:T(8,128)} async-done(((f32[16,16,64,128]{2,1,0,3:T(8,128)}), f32[16,16,64,1]{2,1,0,3:T(8,128)}) %reduce-scatter.2.cloned.1.call-update) | async-done | bytes 65552 | tf_op jit(solution)/shard_map/reduce_scatter | solution.py:42
  847.5 5.5 broadcast_multiply_fusion
  853.2 166.2 %all-reduce.4.cloned.1.call-done = f32[16,16,64,64]{3,2,1,0:T(8,128)} async-done(((f32[16,16,64,64]{3,2,1,0:T(8,128)}), f32[16,16,64,64]{3,2,1,0:T(8,128)}) %all-reduce.4.cloned.1.call-update) | async-done | bytes 4194320 | tf_op jit(solution)/shard_map/psum | solution.py:32
  1019.3 6.6 fusion.9
  1026.2 64.1 %all-reduce = f32[8192]{0:T(1024)S(1)} all-reduce(f32[8192]{0:T(1024)S(1)} %dynamic-update-slice.6), channel_id=2, replica_groups=mesh['gy'=32,'var'=4] {'gy','var'}, use_global_device_ids=true, to_apply=%add | all-reduce | flops 8192 | bytes 65536
  1090.7 5.8 cholesky.29
  1096.6 0.6 compare_reduce_fusion.1
  1097.3 0.7 fusion.13
  1097.9 4.9 custom-call.14
  1102.8 0.3 fusion.16
  1103.1 6.6 fusion.14
  1109.7 4.7 reshape.38
  1114.5 0.9 fusion.29
  1115.4 103.7 %all-reduce.6.cloned.1.call-done = f32[8,65536]{1,0:T(8,128)} async-done(((f32[8,65536]{1,0:T(8,128)}), f32[8,65536]{1,0:T(8,128)}) %all-reduce.6.cloned.1.call-update) | async-done | bytes 2097168 | tf_op jit(solution)/shard_map/psum | solution.py:53
  1219.2 1.2 collective-permute-start
  1220.3 1.6 collective-permute-start.1
  1222.0 0.5 broadcast_in_dim.7
  1222.7 44.4 %collective-permute-done = f32[8,65536]{1,0:T(8,128)S(1)} collective-permute-done((f32[8,65536]{1,0:T(8,128)}, f32[8,65536]{1,0:T(8,128)S(1)}, u32[]{:S(2)}, u32[]{:S(2)}) %collective-permute-start) | collective-permute-done | bytes 2097184 | tf_op jit(solution)/shard_map/ppermute | solution.py:15
  1267.5 46.4 %collective-permute-done.2 = f32[8,65536]{1,0:T(8,128)S(1)} collective-permute-done((f32[8,65536]{1,0:T(8,128)S(1)}, f32[8,65536]{1,0:T(8,128)S(1)}, u32[]{:S(2)}, u32[]{:S(2)}) %collective-permute-start.2) | collective-permute-done | bytes 2097184 | tf_op jit(solution)/shard_map/ppermute | solution.py:15
  1314.1 6.6 fusion.30
  1321.1 1.5 cholesky.61
  1322.6 0.6 compare_reduce_fusion
  1323.2 0.6 fusion.20
  1323.9 1.2 custom-call.15
  1325.3 7.5 fusion.8
  1332.8 0.8 fusion.33
  (37 shorter events, 2.4 us)
Async XLA Ops:
  7.2 172.9 %copy-start = (f32[128,64]{0,1:T(8,128)S(1)}, f32[128,64]{0,1:T(8,128)}, u32[]{:S(2)}) copy-start(f32[128,64]{0,1:T(8,128)} %param.8) | copy-start | bytes 98308
  7.2 840.4 %reduce-scatter.2.cloned.1.call-start = ((), (), s32[]{:S(2)}) async-start(), calls=%async_computation.1 | async-start | bytes 16908288 | tf_op jit(solution)/shard_map/reduce_scatter | solution.py:42
  14.1 12.1 copy-start.5
  18.9 2.0 copy-start.2
  180.0 839.3 %all-reduce.4.cloned.1.call-start = ((), (), s32[]{:S(2)}) async-start(), calls=%async_computation.2 | async-start | bytes 16777216 | tf_op jit(solution)/shard_map/psum | solution.py:32
  847.5 171.8 %copy-start.4 = (f32[16,16,64,1]{2,1,0,3:T(8,128)S(1)}, f32[16,16,64,1]{2,1,0,3:T(8,128)}, u32[]{:S(2)}) copy-start(f32[16,16,64,1]{2,1,0,3:T(8,128)} %reduce-scatter.2.cloned.1.call-done) | copy-start | bytes 196612
  853.1 366.1 %all-reduce.6.cloned.1.call-start = ((), (), s32[]{:S(2)}) async-start(), calls=%async_computation.3 | async-start | bytes 4194304 | tf_op jit(solution)/shard_map/psum | solution.py:53
  1219.2 3.4 copy-start.3
  1219.2 47.9 %collective-permute-start = (f32[8,65536]{1,0:T(8,128)}, f32[8,65536]{1,0:T(8,128)S(1)}, u32[]{:S(2)}, u32[]{:S(2)}) collective-permute-start(f32[8,65536]{1,0:T(8,128)} %all-reduce.6.cloned.1.call-done), channel_id=1, source_target_pairs={{0,1},{1,2},{2,3},{3,0},{4,5},{5,6},{6,7},{7,4},{8,9},{9,10},{10,1... | collective-permute-start | bytes 6291464 | tf_op jit(solution)/shard_map/ppermute | solution.py:15
  1220.3 46.9 %collective-permute-start.1 = (f32[8,65536]{1,0:T(8,128)}, f32[8,65536]{1,0:T(8,128)S(1)}, u32[]{:S(2)}, u32[]{:S(2)}) collective-permute-start(f32[8,65536]{1,0:T(8,128)} %all-reduce.6.cloned.1.call-done), channel_id=1, source_target_pairs={{0,3},{1,0},{2,1},{3,2},{4,7},{5,4},{6,5},{7,6},{8,11},{9,8},{10,9... | collective-permute-start | bytes 6291464 | tf_op jit(solution)/shard_map/ppermute | solution.py:18
  1267.1 46.8 %collective-permute-start.2 = (f32[8,65536]{1,0:T(8,128)S(1)}, f32[8,65536]{1,0:T(8,128)S(1)}, u32[]{:S(2)}, u32[]{:S(2)}) collective-permute-start(f32[8,65536]{1,0:T(8,128)S(1)} %collective-permute-done), channel_id=1, source_target_pairs={{0,1},{1,2},{2,3},{3,0},{4,5},{5,6},{6,7},{7,4},{8,9},{9,10},{10,1... | collective-permute-start | bytes 6291464 | tf_op jit(solution)/shard_map/ppermute | solution.py:15
  1314.1 6.6 copy-start.1
Sparse Core Ops, SparseCore 0:
  180.1 667.3 reduce-scatter.1
  853.2 166.0 all-reduce.3
  1114.5 104.5 all-reduce.5
